TPU v7x, 32 devices: a whole 2x2x4 slice. The times are simulated.
32 devices in a mesh: frame: 8 (over y, x, core), head: 4 (over z).
Axes of the slice: x: 2, y: 2, z: 4, core: 2. Of those that a mesh axis runs over, the one named last changes fastest.
Arguments:
- queries: bfloat16 [4, 2048, 4096], P(None, 'frame', 'head'), may hold values from -6 to 6
- keys: bfloat16 [4, 2048, 4096], P(None, 'frame', 'head'), may hold values from -6 to 6
- values: bfloat16 [4, 2048, 4096], P(None, 'frame', 'head'), may hold values from -6 to 6
- step_sizes: bfloat16 [4, 2048, 16], P(None, 'frame', 'head'), may hold values from 9e-05 to 1.25, as said below
- starts: int32 [4], replicated, may hold values from 0 to 7, as said below
- resets: int32 [4, 8], replicated, may hold values 0 or 1
- init_in: bfloat16 [16, 256, 1024], P('head'), may hold values from -0.375 to 0.375
- init_out: bfloat16 [16, 512, 256], P('head'), may hold values from -0.25 to 0.25
- gain: float32 [4096], P('head'), may hold values from 0.25 to 1.75
- out_proj: bfloat16 [4096, 5120], P('head'), may hold values from -0.125 to 0.125
Outputs:
- mixed_out: bfloat16 [4, 2048, 5120], P(None, 'frame', 'head')
Inputs may be any that keep to these rules, and one draw needn't show every extreme that they name: `starts`: 4 distinct blocks. `step_sizes`: positive.
All inputs are finite; a program needn't handle non-finite values.
Results may differ from a plain program's by a relative error of at most 0.035.
Values may be sent and summed in bfloat16 or wider, within the bound.
No kernel may reach another device: no remote copies, remote signals or barrier semaphores. Data moves between devices by JAX's collectives and lax.ppermute only.
A program may use at most 128 MiB of HBM per device.

v0:
```python
import jax
import jax.numpy as jnp
from jax import lax
from jax.sharding import PartitionSpec as P


def renorm(raw_weights, target):
    column_scale = target[:, None, :] * lax.rsqrt(
        jnp.sum(raw_weights * raw_weights, axis=1, keepdims=True) + 1e-06
    )
    return (raw_weights * column_scale).astype(jnp.bfloat16)


def advance(
    weights_in, weights_out, queries_seg, keys_seg, values_seg, rates_seg, norm_in, norm_out, gain
):
    rows_here = queries_seg.shape[0]
    heads_here = weights_in.shape[0]
    head_width = weights_in.shape[1]
    hidden_width = weights_out.shape[1]
    key_heads = keys_seg.reshape(rows_here, heads_here, head_width)
    pre_keys = jnp.einsum("thd,hde->hte", key_heads, weights_in, preferred_element_type=jnp.float32)
    first_half = pre_keys[..., :hidden_width]
    second_half = pre_keys[..., hidden_width:]
    sigmoid_first = jax.nn.sigmoid(first_half)
    activated = first_half * sigmoid_first
    hidden = (activated * second_half).astype(jnp.bfloat16)
    value_heads = values_seg.reshape(rows_here, heads_here, head_width).astype(jnp.float32)
    scaled = (value_heads * rates_seg.astype(jnp.float32)[:, :, None]).astype(jnp.bfloat16)
    grad_hidden = jnp.einsum(
        "the,hfe->htf", scaled, weights_out, preferred_element_type=jnp.float32
    )
    grad_first = (
        grad_hidden * second_half * sigmoid_first * (1.0 + first_half * (1.0 - sigmoid_first))
    )
    grad_second = grad_hidden * activated
    grad_pre = jnp.concatenate([grad_first, grad_second], axis=-1).astype(jnp.bfloat16)
    raw_in = weights_in.astype(jnp.float32) + jnp.einsum(
        "thd,hte->hde", key_heads, grad_pre, preferred_element_type=jnp.float32
    )
    raw_out = weights_out.astype(jnp.float32) + jnp.einsum(
        "htf,the->hfe", hidden, scaled, preferred_element_type=jnp.float32
    )
    new_in = renorm(raw_in, norm_in)
    new_out = renorm(raw_out, norm_out)
    query_heads = queries_seg.reshape(rows_here, heads_here, head_width)
    pre_queries = jnp.einsum(
        "thd,hde->hte", query_heads, new_in, preferred_element_type=jnp.float32
    )
    hidden_queries = (
        jax.nn.silu(pre_queries[..., :hidden_width]) * pre_queries[..., hidden_width:]
    ).astype(jnp.bfloat16)
    fast_out = jnp.einsum(
        "htf,hfe->the", hidden_queries, new_out, preferred_element_type=jnp.float32
    )
    normed = fast_out * lax.rsqrt(jnp.mean(fast_out * fast_out, axis=-1, keepdims=True) + 1e-05)
    normed = normed * gain.reshape(heads_here, head_width)
    return (
        new_in,
        new_out,
        normed.reshape(rows_here, heads_here * head_width).astype(jnp.bfloat16),
    )


def shards(queries, keys, values, step_sizes, starts, resets, init_in, init_out, gain, out_proj):
    frames = lax.axis_size("frame")
    position = lax.axis_index("frame")
    videos = queries.shape[0]
    rows_block = queries.shape[1]
    norm_in = jnp.sqrt(jnp.sum(jnp.square(init_in.astype(jnp.float32)), axis=1))
    norm_out = jnp.sqrt(jnp.sum(jnp.square(init_out.astype(jnp.float32)), axis=1))
    padding = ((0, frames - videos), (0, 0), (0, 0))
    moved_queries, moved_keys, moved_values, moved_rates = (
        lax.all_to_all(jnp.pad(queries, padding), "frame", split_axis=0, concat_axis=1, tiled=True),
        lax.all_to_all(jnp.pad(keys, padding), "frame", split_axis=0, concat_axis=1, tiled=True),
        lax.all_to_all(jnp.pad(values, padding), "frame", split_axis=0, concat_axis=1, tiled=True),
        lax.all_to_all(
            jnp.pad(step_sizes, padding), "frame", split_axis=0, concat_axis=1, tiled=True
        ),
    )
    video_here = jnp.minimum(position, videos - 1)
    first_block = starts[video_here]
    reset_flags = resets[video_here]

    def local_segment(seg_index, loop_state):
        state_in, state_out, collected = loop_state
        block_now = (first_block + seg_index) % frames
        first_row = block_now * rows_block
        queries_seg = lax.dynamic_slice_in_dim(moved_queries[0], first_row, rows_block, 0)
        keys_seg = lax.dynamic_slice_in_dim(moved_keys[0], first_row, rows_block, 0)
        values_seg = lax.dynamic_slice_in_dim(moved_values[0], first_row, rows_block, 0)
        rates_seg = lax.dynamic_slice_in_dim(moved_rates[0], first_row, rows_block, 0)
        restart = jnp.logical_or(seg_index == 0, reset_flags[seg_index] == 1)
        weights_in = jnp.where(restart, init_in, state_in)
        weights_out = jnp.where(restart, init_out, state_out)
        new_in, new_out, normed = advance(
            weights_in,
            weights_out,
            queries_seg,
            keys_seg,
            values_seg,
            rates_seg,
            norm_in,
            norm_out,
            gain,
        )
        collected = lax.dynamic_update_slice_in_dim(collected, normed, first_row, 0)
        return (new_in, new_out, collected)

    empty_rows = jnp.zeros((moved_queries.shape[1], moved_queries.shape[2]), jnp.bfloat16)
    _, _, own_rows = lax.fori_loop(0, frames, local_segment, (init_in, init_out, empty_rows))
    returned = lax.all_to_all(own_rows[None], "frame", split_axis=1, concat_axis=0, tiled=True)
    normed_all = returned[:videos]
    flat_rows = normed_all.reshape(videos * rows_block, normed_all.shape[2])
    partial_value = jnp.dot(flat_rows, out_proj, preferred_element_type=jnp.float32)
    mixed_out = lax.psum_scatter(
        partial_value.astype(jnp.bfloat16), "head", scatter_dimension=1, tiled=True
    ).astype(jnp.float32)
    return mixed_out.astype(jnp.bfloat16).reshape(videos, rows_block, mixed_out.shape[1])


def solution(mesh):
    return jax.shard_map(
        shards,
        mesh=mesh,
        in_specs=(
            P(None, "frame", "head"),
            P(None, "frame", "head"),
            P(None, "frame", "head"),
            P(None, "frame", "head"),
            P(),
            P(),
            P("head", None, None),
            P("head", None, None),
            P("head"),
            P("head", None),
        ),
        out_specs=P(None, "frame", "head"),
        check_vma=False,
    )
```

profile of v0, /device:TPU:0, one launch (start us, length us, event | category | flops | bytes accessed | tf_op | source)
XLA Modules:
  0.0 665.5 jit_solution(5543504575499884247)
XLA Ops:
  6.5 1.3 pad.16
  7.9 5.2 all-to-all-start.2
  13.1 4.1 pad.17
  17.8 4.6 all-to-all-start.3
  22.4 2.5 pad.14
  24.9 46.6 %all-to-all-done.3 = bf16[8,256,1024]{2,1,0:T(8,128)(2,1)} async-done(((bf16[8,256,1024]{2,1,0:T(8,128)(2,1)}), bf16[8,256,1024]{2,1,0:T(8,128)(2,1)}, u32[]{:S(2)}, u32[]{:S(2)}) %all-to-all-start.3) | async-done | bytes 4194336 | tf_op jit(solution)/shard_map/all_to_all | solution.py:74
  71.5 4.6 all-to-all-start
  76.1 2.4 pad.15
  78.5 46.7 %all-to-all-done = bf16[8,256,1024]{2,1,0:T(8,128)(2,1)} async-done(((bf16[8,256,1024]{2,1,0:T(8,128)(2,1)}), bf16[8,256,1024]{2,1,0:T(8,128)(2,1)}, u32[]{:S(2)}, u32[]{:S(2)}) %all-to-all-start) | async-done | bytes 4194336 | tf_op jit(solution)/shard_map/all_to_all | solution.py:75
  125.1 4.6 all-to-all-start.1
  131.1 1.7 copy.77
  134.6 44.3 %all-to-all-done.1 = bf16[8,256,1024]{2,1,0:T(8,128)(2,1)} async-done(((bf16[8,256,1024]{2,1,0:T(8,128)(2,1)}), bf16[8,256,1024]{2,1,0:T(8,128)(2,1)}, u32[]{:S(2)}, u32[]{:S(2)}) %all-to-all-start.1) | async-done | bytes 4194336 | tf_op jit(solution)/shard_map/all_to_all | solution.py:76
  178.8 2.5 broadcast_in_dim.24
  181.3 158.4 %while.20 = (s32[]{:T(128)}, bf16[4,256,1024]{2,1,0:T(8,128)(2,1)S(1)}, bf16[4,512,256]{2,1,0:T(8,128)(2,1)}, bf16[2048,1024]{0,1:T(8,128)(2,1)}, s32[8]{0:T(128...) while((s32[]{:T(128)}, ...), condition=%wide.wide.region_6.7_spmd, body=%wide.wide.region_2.6_spmd.sunk | while | flops 2449480704 | bytes 95033920 | solution.py:111
  183.3 1.1 constant_dynamic-slice_fusion.4
  184.5 2.4 dynamic-slice_convert_fusion.3
  186.9 2.7 reshape.137
  190.6 1.9 broadcast_select_fusion.5
  194.4 1.6 multiply_convert_fusion.15
  195.9 1.4 multiply_reduce_fusion.12
  204.4 1.1 constant_dynamic-slice_fusion.4
  205.7 2.4 dynamic-slice_convert_fusion.3
  208.1 2.7 reshape.137
  210.8 1.0 copy.74
  214.0 1.5 multiply_convert_fusion.15
  215.5 1.4 multiply_reduce_fusion.12
  224.1 1.1 constant_dynamic-slice_fusion.4
  225.3 2.4 dynamic-slice_convert_fusion.3
  227.7 2.7 reshape.137
  233.6 1.6 multiply_convert_fusion.15
  235.2 1.4 multiply_reduce_fusion.12
  243.6 1.1 constant_dynamic-slice_fusion.4
  244.9 2.4 dynamic-slice_convert_fusion.3
  247.3 2.7 reshape.137
  253.2 1.6 multiply_convert_fusion.15
  254.7 1.4 multiply_reduce_fusion.12
  263.2 1.1 constant_dynamic-slice_fusion.4
  264.5 2.4 dynamic-slice_convert_fusion.3
  266.9 2.7 reshape.137
  272.7 1.6 multiply_convert_fusion.15
  274.3 1.4 multiply_reduce_fusion.12
  282.8 1.1 constant_dynamic-slice_fusion.4
  284.1 2.4 dynamic-slice_convert_fusion.3
  286.5 2.7 reshape.137
  292.3 1.6 multiply_convert_fusion.15
  293.9 1.4 multiply_reduce_fusion.12
  302.4 1.1 constant_dynamic-slice_fusion.4
  303.7 2.4 dynamic-slice_convert_fusion.3
  306.1 2.7 reshape.137
  312.0 1.5 multiply_convert_fusion.15
  313.5 1.4 multiply_reduce_fusion.12
  322.0 1.1 constant_dynamic-slice_fusion.4
  323.3 2.4 dynamic-slice_convert_fusion.3
  325.7 2.7 reshape.137
  331.6 1.6 multiply_convert_fusion.15
  333.1 1.4 multiply_reduce_fusion.12
  339.7 20.5 %copy.42 = bf16[1,2048,1024]{2,0,1:T(2,128)(2,1)} copy(bf16[1,2048,1024]{1,2,0:T(8,128)(2,1)} %bitcast.69) | data formatting | bytes 8388608 | tf_op jit(solution)/shard_map/broadcast_in_dim | solution.py:112
  360.7 26.0 %reduce = bf16[2048,1024]{1,0:T(8,128)(2,1)} reduce(bf16[2048,1,1024]{2,1,0:T(2,128)(2,1)} %bitcast.67, bf16[]{:T(256)} %broadcast.99), dimensions={1}, to_apply=%bitcast.20.reduce_sub_computation | reduce | bytes 8388610
  386.7 7.8 %reshape.133 = bf16[8,2,131072]{2,1,0:T(2,128)(2,1)} reshape(bf16[2048,1024]{1,0:T(8,128)(2,1)} %reduce) | data formatting | bytes 8388608
  394.5 54.2 %all_to_all.60 = bf16[8,2,131072]{2,1,0:T(2,128)(2,1)} all-to-all(bf16[8,2,131072]{2,1,0:T(2,128)(2,1)} %reshape.133), channel_id=1, replica_groups=mesh['frame'=8,'head'=4] {'frame'}, dimensions={0} | all-to-all | bytes 8388608 | tf_op jit(solution)/shard_map/all_to_all | solution.py:112
  448.7 8.8 %reshape.134 = bf16[2048,1,1024]{2,1,0:T(2,128)(2,1)} reshape(bf16[8,2,131072]{2,1,0:T(2,128)(2,1)} %all_to_all.60) | data formatting | bytes 8388608
  457.4 5.1 copy.53
  462.7 17.2 %convolution_convert_fusion = bf16[1024,5120]{1,0:T(8,128)(2,1)} fusion(bf16[1024,1024]{1,0:T(8,128)(2,1)S(1)} %bitcast.71, bf16[1024,5120]{1,0:T(8,128)(2,1)} %param.21), kind=kOutput, calls=%fused_computation.36 | convolution fusion | flops 10742661120 | bytes 23068672 | tf_op jit(solution)/shard_map/dot_general | solution.py:115
  480.0 178.6 %reduce-scatter.2.cloned.1.call-done = bf16[1024,1280]{1,0:T(8,128)(2,1)} async-done(((bf16[1024,5120]{1,0:T(8,128)(2,1)}), bf16[1024,1280]{1,0:T(8,128)(2,1)}) %reduce-scatter.2.cloned.1.call-update) | async-done | bytes 2621456 | tf_op jit(solution)/shard_map/reduce_scatter | solution.py:116
  (235 shorter events, 75.2 us)
Async XLA Ops:
  6.5 128.0 %copy-start = (s32[4,8]{1,0:T(4,128)S(1)}, s32[4,8]{1,0:T(4,128)}, u32[]{:S(2)}) copy-start(s32[4,8]{1,0:T(4,128)} %param.17) | copy-start | bytes 388
  7.9 10.0 %all-to-all-start.2 = ((bf16[8,256,4]{1,2,0:T(4,128)(2,1)}), bf16[8,256,4]{1,2,0:T(4,128)(2,1)S(1)}, u32[]{:S(2)}, u32[]{:S(2)}) async-start(bf16[8,256,4]{1,2,0:T(4,128)(2,1)} %pad.16), calls=%async_computation.2 | async-start | bytes 32768 | tf_op jit(solution)/shard_map/all_to_all | solution.py:77
  17.1 5.3 copy-start.7
  17.8 53.7 %all-to-all-start.3 = ((bf16[8,256,1024]{2,1,0:T(8,128)(2,1)}), bf16[8,256,1024]{2,1,0:T(8,128)(2,1)}, u32[]{:S(2)}, u32[]{:S(2)}) async-start(bf16[8,256,1024]{2,1,0:T(8,128)(2,1)} %pad.17), calls=%async_computation.3 | async-start | bytes 8388608 | tf_op jit(solution)/shard_map/all_to_all | solution.py:74
  24.9 51.2 %copy-start.8 = (bf16[4,256,1024]{2,1,0:T(8,128)(2,1)S(1)}, bf16[4,256,1024]{2,1,0:T(8,128)(2,1)}, u32[]{:S(2)}) copy-start(bf16[4,256,1024]{2,1,0:T(8,128)(2,1)} %param.14) | copy-start | bytes 6291460
  71.5 53.7 %all-to-all-start = ((bf16[8,256,1024]{2,1,0:T(8,128)(2,1)}), bf16[8,256,1024]{2,1,0:T(8,128)(2,1)}, u32[]{:S(2)}, u32[]{:S(2)}) async-start(bf16[8,256,1024]{2,1,0:T(8,128)(2,1)} %pad.14), calls=%async_computation | async-start | bytes 8388608 | tf_op jit(solution)/shard_map/all_to_all | solution.py:75
  78.5 51.3 %copy-start.11 = (f32[1024]{0:T(1024)S(1)}, f32[1024]{0:T(1024)}, u32[]{:S(2)}) copy-start(f32[1024]{0:T(1024)} %param.20) | copy-start | bytes 12292
  78.5 51.3 %copy-start.5 = (bf16[4,512,256]{2,1,0:T(8,128)(2,1)S(1)}, bf16[4,512,256]{2,1,0:T(8,128)(2,1)}, u32[]{:S(2)}) copy-start(bf16[4,512,256]{2,1,0:T(8,128)(2,1)} %param.19) | copy-start | bytes 3145732
  125.1 53.7 %all-to-all-start.1 = ((bf16[8,256,1024]{2,1,0:T(8,128)(2,1)}), bf16[8,256,1024]{2,1,0:T(8,128)(2,1)}, u32[]{:S(2)}, u32[]{:S(2)}) async-start(bf16[8,256,1024]{2,1,0:T(8,128)(2,1)} %pad.15), calls=%async_computation.1 | async-start | bytes 8388608 | tf_op jit(solution)/shard_map/all_to_all | solution.py:76
  129.7 528.9 %reduce-scatter.2.cloned.1.call-start = ((), (), s32[]{:S(2)}) async-start(), calls=%async_computation.6 | async-start | bytes 13107200 | tf_op jit(solution)/shard_map/reduce_scatter | solution.py:116
  131.0 2.2 copy-start.2
  133.3 0.7 copy-start.12
  192.5 1.2 copy-start.4
  192.5 1.5 copy-start.6
  192.5 1.8 copy-start.9
  197.6 2.8 copy-start.10
  198.6 1.0 copy-start.3
  212.1 1.2 copy-start.4
  212.1 1.5 copy-start.6
  212.1 1.8 copy-start.9
  217.2 2.8 copy-start.10
  218.2 1.0 copy-start.3
  231.7 1.2 copy-start.4
  231.7 1.5 copy-start.6
  231.8 1.8 copy-start.9
  236.8 2.8 copy-start.10
  237.8 1.0 copy-start.3
  251.3 1.2 copy-start.4
  251.3 1.5 copy-start.6
  251.3 1.8 copy-start.9
  256.4 2.8 copy-start.10
  257.4 1.0 copy-start.3
  270.9 1.2 copy-start.4
  270.9 1.5 copy-start.6
  270.9 1.8 copy-start.9
  275.9 2.8 copy-start.10
  277.0 1.0 copy-start.3
  290.5 1.2 copy-start.4
  290.5 1.5 copy-start.6
  290.5 1.8 copy-start.9
  295.5 2.8 copy-start.10
  296.6 1.0 copy-start.3
  310.1 1.2 copy-start.4
  310.1 1.5 copy-start.6
  310.1 1.8 copy-start.9
  315.2 2.8 copy-start.10
  316.2 1.0 copy-start.3
  329.7 1.2 copy-start.4
  329.7 1.5 copy-start.6
  329.7 1.8 copy-start.9
  334.8 2.8 copy-start.10
  335.8 1.0 copy-start.3
  480.0 178.6 %copy-start.1 = (s32[4,8]{1,0:T(4,128)S(1)}, s32[4,8]{1,0:T(4,128)}, u32[]{:S(2)}) copy-start(s32[4,8]{1,0:T(4,128)} %param.17) | copy-start | bytes 388
Sparse Core Ops, SparseCore 0:
  480.1 178.4 reduce-scatter.1
where the time goes:
time: 669 us; the launch traced here: 665 us
  waiting for transfers between devices  317 us (47%)
  local copies, waits for them, and re-layouts  122 us (18%)
  matrix products  68.7 us (10%)
  other arithmetic  59.4 us (9%)
  blocking collectives  54.2 us (8%)
  starting transfers between devices  19 us (3%)
  between operations  13.5 us (2%)
  loops' own time  11.9 us (2%)
    reduce_scatter x1, waiting for transfers between devices, shards(): lax.psum_scatter(partial_value.astype(jnp.bfloat16), 'head', scatter_dime...  179 us
    all_to_all x1, blocking collectives, shards(): lax.all_to_all(own_rows[None], 'frame', split_axis=1, concat_axis=0, tile...  54.2 us
    all_to_all x1, waiting for transfers between devices, shards(): lax.all_to_all(jnp.pad(keys, padding), 'frame', split_axis=0, concat_axis...  46.7 us
    all_to_all x1, waiting for transfers between devices, shards(): lax.all_to_all(jnp.pad(queries, padding), 'frame', split_axis=0, concat_a...  46.6 us
    all_to_all x1, waiting for transfers between devices, shards(): lax.all_to_all(jnp.pad(values, padding), 'frame', split_axis=0, concat_ax...  44.3 us
    unnamed x1, other arithmetic  26 us
    unnamed x22, local copies, waits for them, and re-layouts  25.5 us
    convert_element_type x8, local copies, waits for them, and re-layouts, advance(): values_seg.reshape(rows_here, heads_here, head_width).astype(jnp.float32)  21.3 us
  transfers between devices with their start and end apart: 5, of which 5 were waited for; matrix products, arithmetic and copies ran while one was open for 2% of the time, Pallas kernels for 0%

commit v1 on v0

--- a/solution.py
+++ b/solution.py
@@ -2,6 +2,18 @@
 import jax.numpy as jnp
 from jax import lax
 from jax.sharding import PartitionSpec as P
+
+
+def split_up(x, dim, length):
+    dims = x.shape
+    blocks = x.reshape(*dims[:dim], length, dims[dim] // length, *dims[dim + 1 :])
+    return jnp.moveaxis(blocks, dim, 0)
+
+
+def laid_out(pieces, dim):
+    pieces = jnp.moveaxis(pieces, 0, dim)
+    shape = pieces.shape
+    return pieces.reshape(*shape[:dim], shape[dim] * shape[dim + 1], *shape[dim + 2 :])
 
 
 def renorm(raw_weights, target):
@@ -109,7 +121,14 @@
 
     empty_rows = jnp.zeros((moved_queries.shape[1], moved_queries.shape[2]), jnp.bfloat16)
     _, _, own_rows = lax.fori_loop(0, frames, local_segment, (init_in, init_out, empty_rows))
-    returned = lax.all_to_all(own_rows[None], "frame", split_axis=1, concat_axis=0, tiled=True)
+    size, index = (lax.axis_size("frame"), lax.axis_index("frame"))
+    parts = split_up(own_rows[None], 1, size)
+    done = [parts[index]]
+    for step in range(1, size):
+        sent = parts[index ^ step]
+        done.append(lax.ppermute(sent, "frame", [(i, i ^ step) for i in range(size)]))
+    parts = jnp.stack(done)[index ^ jnp.arange(size)]
+    returned = laid_out(parts, 0)
     normed_all = returned[:videos]
     flat_rows = normed_all.reshape(videos * rows_block, normed_all.shape[2])
     partial_value = jnp.dot(flat_rows, out_proj, preferred_element_type=jnp.float32)

time: 669 us -> 612 us (0.915)
  blocking collectives: 54.2 us -> 0 us
  waiting for transfers between devices: 317 us -> 357 us
  local copies, waits for them, and re-layouts: 122 us -> 95.8 us
  other arithmetic: 59.4 us -> 34.9 us
  starting transfers between devices: 19 us -> 28.1 us
    all_to_all x1 -> x0, blocking collectives: 54.2 us -> none  [shards(): lax.all_to_all(own_rows[None], 'frame', split_axis=1, concat_axis=0, tile...]
    ppermute x0 -> x7, waiting for transfers between devices: none -> 40.9 us  [shards(): lax.ppermute(sent, 'frame', [(i, i ^ step) for i in range(size)])]
    unnamed x1 -> x0, other arithmetic: 26 us -> none
    broadcast_in_dim x1 -> x0, local copies, waits for them, and re-layouts: 20.5 us -> none  [shards(): own_rows[None]]
    unnamed x22, local copies, waits for them, and re-layouts: 25.5 us -> 7.57 us
    ppermute x0 -> x7, starting transfers between devices: none -> 9.19 us  [shards(): lax.ppermute(sent, 'frame', [(i, i ^ step) for i in range(size)])]
  transfers between devices with their start and end apart: 5 -> 12, of which waited for: 5 -> 8; matrix products, arithmetic and copies ran while one was open for 2% -> 3% of each run, Pallas kernels for 0% -> 0%
where the time goes in v1:
time: 612 us; the launch traced here: 609 us
  waiting for transfers between devices  357 us (58%)
  local copies, waits for them, and re-layouts  95.8 us (16%)
  matrix products  68.1 us (11%)
  other arithmetic  34.9 us (6%)
  starting transfers between devices  28.1 us (5%)
  between operations  13.6 us (2%)
  loops' own time  11.5 us (2%)
    reduce_scatter x1, waiting for transfers between devices, shards(): lax.psum_scatter(partial_value.astype(jnp.bfloat16), 'head', scatter_dime...  179 us
    all_to_all x1, waiting for transfers between devices, shards(): lax.all_to_all(jnp.pad(keys, padding), 'frame', split_axis=0, concat_axis...  46.6 us
    all_to_all x1, waiting for transfers between devices, shards(): lax.all_to_all(jnp.pad(queries, padding), 'frame', split_axis=0, concat_a...  46.6 us
    all_to_all x1, waiting for transfers between devices, shards(): lax.all_to_all(jnp.pad(values, padding), 'frame', split_axis=0, concat_ax...  43.4 us
    ppermute x7, waiting for transfers between devices, shards(): lax.ppermute(sent, 'frame', [(i, i ^ step) for i in range(size)])  40.9 us
    convert_element_type x8, local copies, waits for them, and re-layouts, advance(): values_seg.reshape(rows_here, heads_here, head_width).astype(jnp.float32)  21.4 us
    convert_element_type x8, other arithmetic, advance(): values_seg.reshape(rows_here, heads_here, head_width).astype(jnp.float32)  18.4 us
    dot_general x1, matrix products, shards(): jnp.dot(flat_rows, out_proj, preferred_element_type=jnp.float32)  17.3 us
  transfers between devices with their start and end apart: 12, of which 8 were waited for; matrix products, arithmetic and copies ran while one was open for 3% of the time, Pallas kernels for 0%

profile of v1, /device:TPU:0, one launch (start us, length us, event | category | flops | bytes accessed | tf_op | source)
XLA Modules:
  0.0 609.3 jit_solution(15234268988315962117)
XLA Ops:
  6.5 1.3 pad.16
  7.9 5.2 all-to-all-start.2
  13.1 4.1 pad.17
  17.8 4.6 all-to-all-start.3
  22.4 2.5 pad.14
  24.9 46.6 %all-to-all-done.3 = bf16[8,256,1024]{2,1,0:T(8,128)(2,1)} async-done(((bf16[8,256,1024]{2,1,0:T(8,128)(2,1)}), bf16[8,256,1024]{2,1,0:T(8,128)(2,1)}, u32[]{:S(2)}, u32[]{:S(2)}) %all-to-all-start.3) | async-done | bytes 4194336 | tf_op jit(solution)/shard_map/all_to_all | solution.py:86
  71.5 4.6 all-to-all-start
  76.0 2.5 pad.15
  78.5 46.6 %all-to-all-done = bf16[8,256,1024]{2,1,0:T(8,128)(2,1)} async-done(((bf16[8,256,1024]{2,1,0:T(8,128)(2,1)}), bf16[8,256,1024]{2,1,0:T(8,128)(2,1)}, u32[]{:S(2)}, u32[]{:S(2)}) %all-to-all-start) | async-done | bytes 4194336 | tf_op jit(solution)/shard_map/all_to_all | solution.py:87
  125.1 4.6 all-to-all-start.1
  131.1 1.6 copy.72
  132.7 2.0 multiply_reduce_fusion.3
  135.4 43.4 %all-to-all-done.1 = bf16[8,256,1024]{2,1,0:T(8,128)(2,1)} async-done(((bf16[8,256,1024]{2,1,0:T(8,128)(2,1)}), bf16[8,256,1024]{2,1,0:T(8,128)(2,1)}, u32[]{:S(2)}, u32[]{:S(2)}) %all-to-all-start.1) | async-done | bytes 4194336 | tf_op jit(solution)/shard_map/all_to_all | solution.py:88
  178.8 2.5 broadcast_in_dim.22.clone
  181.3 158.9 %while.20 = (s32[]{:T(128)}, bf16[4,256,1024]{2,1,0:T(8,128)(2,1)S(1)}, bf16[4,512,256]{2,1,0:T(8,128)(2,1)}, bf16[2048,1024]{1,0:T(8,128)(2,1)}, s32[8]{0:T(128...) while((s32[]{:T(128)}, ...), condition=%wide.wide.region_6.7_spmd, body=%wide.wide.region_2.6_spmd.sunk | while | flops 2449480704 | bytes 96082496 | solution.py:123
  183.3 1.1 constant_dynamic-slice_fusion.5
  184.6 2.3 dynamic-slice_convert_fusion.3
  186.9 2.7 reshape.162
  190.6 1.9 broadcast_select_fusion.5
  194.4 1.5 multiply_convert_fusion.15
  195.9 1.4 multiply_reduce_fusion.12
  205.8 2.3 dynamic-slice_convert_fusion.3
  208.1 2.7 reshape.162
  214.0 1.5 multiply_convert_fusion.15
  215.6 1.4 multiply_reduce_fusion.12
  225.5 2.3 dynamic-slice_convert_fusion.3
  227.8 2.7 reshape.162
  233.7 1.5 multiply_convert_fusion.15
  235.2 1.4 multiply_reduce_fusion.12
  243.9 1.1 constant_dynamic-slice_fusion.5
  245.1 2.3 dynamic-slice_convert_fusion.3
  247.5 2.7 reshape.162
  253.3 1.5 multiply_convert_fusion.15
  254.9 1.4 multiply_reduce_fusion.12
  263.5 1.1 constant_dynamic-slice_fusion.5
  264.8 2.3 dynamic-slice_convert_fusion.3
  267.1 2.7 reshape.162
  273.0 1.5 multiply_convert_fusion.15
  274.5 1.4 multiply_reduce_fusion.12
  283.2 1.1 constant_dynamic-slice_fusion.5
  284.5 2.3 dynamic-slice_convert_fusion.3
  286.8 2.7 reshape.162
  292.7 1.5 multiply_convert_fusion.15
  294.2 1.4 multiply_reduce_fusion.12
  302.9 1.1 constant_dynamic-slice_fusion.5
  304.2 2.3 dynamic-slice_convert_fusion.3
  306.5 2.7 reshape.162
  312.4 1.5 multiply_convert_fusion.15
  313.9 1.4 multiply_reduce_fusion.12
  323.8 2.3 dynamic-slice_convert_fusion.3
  326.1 2.7 reshape.162
  332.0 1.5 multiply_convert_fusion.15
  333.6 1.4 multiply_reduce_fusion.12
  340.3 3.4 dynamic-slice_bitcast_fusion
  343.7 3.7 collective-permute-start.1
  347.5 1.7 collective-permute-start.6
  350.2 1.9 collective-permute-start.3
  352.9 7.3 %collective-permute-done.1 = bf16[1,256,1024]{2,1,0:T(8,128)(2,1)S(1)} collective-permute-done((bf16[1,256,1024]{2,1,0:T(8,128)(2,1)S(1)}, bf16[1,256,1024]{2,1,0:T(8,128)(2,1)S(1)}, u32[]{:S(2)}, u32[]{:S(2)}) %collective-permute-start.1) | collective-permute-done | bytes 524320 | tf_op jit(solution)/shard_map/ppermute | solution.py:129
  361.8 9.1 %collective-permute-done.2 = bf16[1,256,1024]{2,1,0:T(8,128)(2,1)S(1)} collective-permute-done((bf16[1,256,1024]{2,1,0:T(8,128)(2,1)S(1)}, bf16[1,256,1024]{2,1,0:T(8,128)(2,1)S(1)}, u32[]{:S(2)}, u32[]{:S(2)}) %collective-permute-start.2) | collective-permute-done | bytes 524320 | tf_op jit(solution)/shard_map/ppermute | solution.py:129
  372.6 24.4 %collective-permute-done.4 = bf16[1,256,1024]{2,1,0:T(8,128)(2,1)S(1)} collective-permute-done((bf16[1,256,1024]{2,1,0:T(8,128)(2,1)S(1)}, bf16[1,256,1024]{2,1,0:T(8,128)(2,1)S(1)}, u32[]{:S(2)}, u32[]{:S(2)}) %collective-permute-start.4) | collective-permute-done | bytes 524320 | tf_op jit(solution)/shard_map/ppermute | solution.py:129
  399.5 5.0 gather_fusion
  404.5 1.6 slice-done
  406.1 17.3 %convolution_convert_fusion = bf16[1024,5120]{1,0:T(8,128)(2,1)} fusion(bf16[1024,1024]{1,0:T(8,128)(2,1)S(1)} %bitcast.110, bf16[1024,5120]{1,0:T(8,128)(2,1)} %param.21), kind=kOutput, calls=%fused_computation.37 | convolution fusion | flops 10742661120 | bytes 23068672 | tf_op jit(solution)/shard_map/dot_general | solution.py:134
  423.4 179.0 %reduce-scatter.2.cloned.1.call-done = bf16[1024,1280]{1,0:T(8,128)(2,1)} async-done(((bf16[1024,5120]{1,0:T(8,128)(2,1)}), bf16[1024,1280]{1,0:T(8,128)(2,1)}) %reduce-scatter.2.cloned.1.call-update) | async-done | bytes 2621456 | tf_op jit(solution)/shard_map/reduce_scatter | solution.py:135
  (260 shorter events, 87.4 us)
Async XLA Ops:
  6.5 128.9 %copy-start = (s32[4,8]{1,0:T(4,128)S(1)}, s32[4,8]{1,0:T(4,128)}, u32[]{:S(2)}) copy-start(s32[4,8]{1,0:T(4,128)} %param.17) | copy-start | bytes 388
  7.9 10.0 %all-to-all-start.2 = ((bf16[8,256,4]{1,2,0:T(4,128)(2,1)}), bf16[8,256,4]{1,2,0:T(4,128)(2,1)S(1)}, u32[]{:S(2)}, u32[]{:S(2)}) async-start(bf16[8,256,4]{1,2,0:T(4,128)(2,1)} %pad.16), calls=%async_computation.2 | async-start | bytes 32768 | tf_op jit(solution)/shard_map/all_to_all | solution.py:89
  17.1 5.2 copy-start.6
  17.8 53.7 %all-to-all-start.3 = ((bf16[8,256,1024]{2,1,0:T(8,128)(2,1)}), bf16[8,256,1024]{2,1,0:T(8,128)(2,1)}, u32[]{:S(2)}, u32[]{:S(2)}) async-start(bf16[8,256,1024]{2,1,0:T(8,128)(2,1)} %pad.17), calls=%async_computation.3 | async-start | bytes 8388608 | tf_op jit(solution)/shard_map/all_to_all | solution.py:86
  24.9 51.2 %copy-start.7 = (bf16[4,256,1024]{2,1,0:T(8,128)(2,1)S(1)}, bf16[4,256,1024]{2,1,0:T(8,128)(2,1)}, u32[]{:S(2)}) copy-start(bf16[4,256,1024]{2,1,0:T(8,128)(2,1)} %param.14) | copy-start | bytes 6291460
  71.5 53.7 %all-to-all-start = ((bf16[8,256,1024]{2,1,0:T(8,128)(2,1)}), bf16[8,256,1024]{2,1,0:T(8,128)(2,1)}, u32[]{:S(2)}, u32[]{:S(2)}) async-start(bf16[8,256,1024]{2,1,0:T(8,128)(2,1)} %pad.14), calls=%async_computation | async-start | bytes 8388608 | tf_op jit(solution)/shard_map/all_to_all | solution.py:87
  78.5 51.3 %copy-start.10 = (f32[1024]{0:T(1024)S(1)}, f32[1024]{0:T(1024)}, u32[]{:S(2)}) copy-start(f32[1024]{0:T(1024)} %param.20) | copy-start | bytes 12292
  78.5 51.3 %copy-start.4 = (bf16[4,512,256]{2,1,0:T(8,128)(2,1)S(1)}, bf16[4,512,256]{2,1,0:T(8,128)(2,1)}, u32[]{:S(2)}) copy-start(bf16[4,512,256]{2,1,0:T(8,128)(2,1)} %param.19) | copy-start | bytes 3145732
  125.1 53.7 %all-to-all-start.1 = ((bf16[8,256,1024]{2,1,0:T(8,128)(2,1)}), bf16[8,256,1024]{2,1,0:T(8,128)(2,1)}, u32[]{:S(2)}, u32[]{:S(2)}) async-start(bf16[8,256,1024]{2,1,0:T(8,128)(2,1)} %pad.15), calls=%async_computation.1 | async-start | bytes 8388608 | tf_op jit(solution)/shard_map/all_to_all | solution.py:88
  129.8 472.7 %reduce-scatter.2.cloned.1.call-start = ((), (), s32[]{:S(2)}) async-start(), calls=%async_computation.5 | async-start | bytes 13107200 | tf_op jit(solution)/shard_map/reduce_scatter | solution.py:135
  130.8 3.9 copy-start.11
  192.5 1.2 copy-start.3
  192.5 1.5 copy-start.5
  192.5 1.8 copy-start.8
  197.5 2.9 copy-start.9
  198.5 1.0 copy-start.2
  212.2 1.2 copy-start.3
  212.2 1.5 copy-start.5
  212.2 1.8 copy-start.8
  217.2 2.9 copy-start.9
  218.2 1.0 copy-start.2
  231.8 1.2 copy-start.3
  231.8 1.5 copy-start.5
  231.8 1.8 copy-start.8
  236.8 2.9 copy-start.9
  237.9 1.0 copy-start.2
  251.5 1.2 copy-start.3
  251.5 1.5 copy-start.5
  251.5 1.8 copy-start.8
  256.5 2.9 copy-start.9
  257.5 1.0 copy-start.2
  271.1 1.2 copy-start.3
  271.1 1.5 copy-start.5
  271.2 1.8 copy-start.8
  276.1 2.9 copy-start.9
  277.2 1.0 copy-start.2
  290.8 1.2 copy-start.3
  290.8 1.5 copy-start.5
  290.8 1.8 copy-start.8
  295.8 2.9 copy-start.9
  296.8 1.0 copy-start.2
  310.5 1.2 copy-start.3
  310.5 1.5 copy-start.5
  310.5 1.8 copy-start.8
  315.5 2.9 copy-start.9
  316.6 1.0 copy-start.2
  330.2 1.2 copy-start.3
  330.2 1.5 copy-start.5
  330.2 1.8 copy-start.8
  335.2 2.9 copy-start.9
  336.2 1.0 copy-start.2
  343.6 6.5 %collective-permute-start = (bf16[1,256,1024]{2,1,0:T(8,128)(2,1)S(1)}, bf16[1,256,1024]{2,1,0:T(8,128)(2,1)S(1)}, u32[]{:S(2)}, u32[]{:S(2)}) collective-permute-start(bf16[1,256,1024]{2,1,0:T(8,128)(2,1)S(1)} %get-tuple-element.405), channel_id=1, source_target_pairs={{0,4},{4,0},{8,12},{12,8},{16,20},{20,16},{24,28},{28,24},{1,5},{5... | collective-permute-start | bytes 1572872 | tf_op jit(solution)/shard_map/ppermute | solution.py:129
  343.7 16.4 %collective-permute-start.1 = (bf16[1,256,1024]{2,1,0:T(8,128)(2,1)S(1)}, bf16[1,256,1024]{2,1,0:T(8,128)(2,1)S(1)}, u32[]{:S(2)}, u32[]{:S(2)}) collective-permute-start(bf16[1,256,1024]{2,1,0:T(8,128)(2,1)S(1)} %get-tuple-element.404), channel_id=1, source_target_pairs={{0,8},{4,12},{8,0},{12,4},{16,24},{20,28},{24,16},{28,20},{1,9},{5... | collective-permute-start | bytes 1572872 | tf_op jit(solution)/shard_map/ppermute | solution.py:129
  347.4 23.5 %collective-permute-start.2 = (bf16[1,256,1024]{2,1,0:T(8,128)(2,1)S(1)}, bf16[1,256,1024]{2,1,0:T(8,128)(2,1)S(1)}, u32[]{:S(2)}, u32[]{:S(2)}) collective-permute-start(bf16[1,256,1024]{2,1,0:T(8,128)(2,1)S(1)} %get-tuple-element.403), channel_id=1, source_target_pairs={{0,12},{4,8},{8,4},{12,0},{16,28},{20,24},{24,20},{28,16},{1,13},{... | collective-permute-start | bytes 1572872 | tf_op jit(solution)/shard_map/ppermute | solution.py:129
  347.5 51.2 %collective-permute-start.6 = (bf16[1,256,1024]{2,1,0:T(8,128)(2,1)S(1)}, bf16[1,256,1024]{2,1,0:T(8,128)(2,1)S(1)}, u32[]{:S(2)}, u32[]{:S(2)}) collective-permute-start(bf16[1,256,1024]{2,1,0:T(8,128)(2,1)S(1)} %get-tuple-element.399), channel_id=1, source_target_pairs={{0,28},{4,24},{8,20},{12,16},{16,12},{20,8},{24,4},{28,0},{1,29},{... | collective-permute-start | bytes 1572872 | tf_op jit(solution)/shard_map/ppermute | solution.py:129
  349.2 48.7 %collective-permute-start.5 = (bf16[1,256,1024]{2,1,0:T(8,128)(2,1)S(1)}, bf16[1,256,1024]{2,1,0:T(8,128)(2,1)S(1)}, u32[]{:S(2)}, u32[]{:S(2)}) collective-permute-start(bf16[1,256,1024]{2,1,0:T(8,128)(2,1)S(1)} %get-tuple-element.400), channel_id=1, source_target_pairs={{0,24},{4,28},{8,16},{12,20},{16,8},{20,12},{24,0},{28,4},{1,25},{... | collective-permute-start | bytes 1572872 | tf_op jit(solution)/shard_map/ppermute | solution.py:129
  350.2 21.6 %collective-permute-start.3 = (bf16[1,256,1024]{2,1,0:T(8,128)(2,1)S(1)}, bf16[1,256,1024]{2,1,0:T(8,128)(2,1)S(1)}, u32[]{:S(2)}, u32[]{:S(2)}) collective-permute-start(bf16[1,256,1024]{2,1,0:T(8,128)(2,1)S(1)} %get-tuple-element.402), channel_id=1, source_target_pairs={{0,16},{4,20},{8,24},{12,28},{16,0},{20,4},{24,8},{28,12},{1,17},{... | collective-permute-start | bytes 1572872 | tf_op jit(solution)/shard_map/ppermute | solution.py:129
  360.2 36.9 %collective-permute-start.4 = (bf16[1,256,1024]{2,1,0:T(8,128)(2,1)S(1)}, bf16[1,256,1024]{2,1,0:T(8,128)(2,1)S(1)}, u32[]{:S(2)}, u32[]{:S(2)}) collective-permute-start(bf16[1,256,1024]{2,1,0:T(8,128)(2,1)S(1)} %get-tuple-element.401), channel_id=1, source_target_pairs={{0,20},{4,16},{8,28},{12,24},{16,4},{20,0},{24,12},{28,8},{1,21},{... | collective-permute-start | bytes 1572872 | tf_op jit(solution)/shard_map/ppermute | solution.py:129
  404.5 1.6 slice-start
  423.4 179.0 %copy-start.1 = (s32[4,8]{1,0:T(4,128)S(1)}, s32[4,8]{1,0:T(4,128)}, u32[]{:S(2)}) copy-start(s32[4,8]{1,0:T(4,128)} %param.17) | copy-start | bytes 388
Sparse Core Ops, SparseCore 0:
  423.6 178.8 reduce-scatter.1
